TPU v7x, 128 devices: a whole 4x4x4 slice. The times are simulated.
128 devices in a mesh: req: 16 (over y, z), mdl: 8 (over x, core).
Axes of the slice: x: 4, y: 4, z: 4, core: 2. Of those that a mesh axis runs over, the one named last changes fastest.
Arguments:
- segments: int32 [1024], P('req'), may hold values from -1 to 1023, as said below
- queries: bfloat16 [1024, 8192], P('req', 'mdl'), may hold values from -200 to 200
- keys_values: bfloat16 [1024, 2, 1024], P('req', None, 'mdl'), may hold values from -6 to 6
- page_table: int32 [64], replicated, may hold values from 0 to 127, as said below
- paged_cache: bfloat16 [128, 16, 2, 1024], P('req', None, None, 'mdl'), may hold values from -6 to 6
- residual: bfloat16 [1024, 8192], P(None, 'req'), may hold values from -40 to 40
- out_weight: bfloat16 [8192, 8192], P('mdl', 'req'), may hold values from -0.0625 to 0.0625
- norm_gain: bfloat16 [8192], P('req'), may hold values from 0.099609375 to 1.8984375
- gate_up_weight: bfloat16 [8192, 2, 29568], P('req', None, 'mdl'), may hold values from -0.0625 to 0.0625
Outputs:
- hidden: bfloat16 [1024, 29568], P('req', 'mdl')
- cache_new: bfloat16 [128, 16, 2, 1024], P('req', None, None, 'mdl')
Inputs may be any that keep to these rules, and one draw needn't show every extreme that they name: `segments`: each block of 64 slots of one index of req holds whole requests followed by pads; a live slot's entry is the slot index of its request's first slot, in that block; in every draw some block has no pads. `page_table`: all entries differ; page p lies on index p // 8 of req; the pages of one block of 64 slots all lie on one index of req, and different blocks on different indices.
All inputs are finite; a program needn't handle non-finite values.
Results may differ from a plain program's by a relative error of at most 0.024.
Values may be sent and summed in bfloat16 or wider, within the bound.
A program may use at most 128 MiB of HBM per device.

v0:
```python
import jax
import jax.numpy as jnp
from jax import lax
from jax.sharding import PartitionSpec as P

D = 8192
HD = 128
QPK = 8
PAGE = 16
EPSILON = 1e-06


def attention_block(query_rows, pair_rows, seg_rows):
    slots = seg_rows.shape[0]
    groups = pair_rows.shape[2] // HD
    query = query_rows.reshape(slots, groups, QPK, HD)
    keys = pair_rows[:, 0].reshape(slots, groups, HD)
    values = pair_rows[:, 1].reshape(slots, groups, HD)
    scores = jnp.einsum("igqd,jgd->gqij", query, keys, preferred_element_type=jnp.float32) * HD ** (
        -0.5
    )
    places = jnp.arange(slots, dtype=jnp.int32)
    allowed = (
        (seg_rows[:, None] == seg_rows[None, :])
        & (seg_rows[:, None] >= 0)
        & (places[None, :] < places[:, None])
    )
    allowed = allowed | (places[:, None] == places[None, :])
    scores = jnp.where(allowed, scores, -jnp.inf)
    highest = jnp.max(scores, axis=-1, keepdims=True)
    weights = jnp.exp(scores - highest)
    probs = (weights / jnp.sum(weights, axis=-1, keepdims=True)).astype(jnp.bfloat16)
    mixed = jnp.einsum("gqij,jgd->igqd", probs, values, preferred_element_type=jnp.float32)
    mixed = jnp.where((seg_rows >= 0)[:, None, None, None], mixed, 0.0)
    return mixed.reshape(slots, groups * QPK * HD).astype(jnp.bfloat16)


def on_device(
    segments,
    queries,
    keys_values,
    page_table,
    paged_cache,
    residual,
    out_weight,
    norm_gain,
    gate_up_weight,
):
    attended = attention_block(queries, keys_values, segments)
    live_rows = (segments >= 0).astype(jnp.bfloat16)
    every_pair, every_live = (
        lax.all_gather(keys_values, "req", axis=0, tiled=True),
        lax.all_gather(live_rows, "req", axis=0, tiled=True),
    )
    local_pages = paged_cache.shape[0]
    slot_count = every_pair.shape[0]
    token_pages = jnp.repeat(page_table, PAGE, total_repeat_length=slot_count)
    target = token_pages - lax.axis_index("req") * local_pages
    writable = (target >= 0) & (target < local_pages) & (every_live > 0)
    target = jnp.where(writable, target, local_pages)
    offsets = jnp.arange(slot_count, dtype=jnp.int32) % PAGE
    cache_new = paged_cache.at[target, offsets].set(every_pair, mode="drop")
    partial_value = jnp.dot(
        lax.all_gather(attended, "req", axis=0, tiled=True),
        out_weight,
        preferred_element_type=jnp.float32,
    )
    gain_row = norm_gain.astype(jnp.float32)
    stream = residual.astype(jnp.float32) + lax.psum(
        partial_value.astype(jnp.bfloat16), "mdl"
    ).astype(jnp.float32)
    squares = jnp.sum(stream * stream, axis=1)
    totals = lax.psum(squares, "req")
    normed = (stream * lax.rsqrt(totals / D + EPSILON)[:, None] * gain_row[None, :]).astype(
        jnp.bfloat16
    )
    flat_weight = gate_up_weight.reshape(gate_up_weight.shape[0], -1)
    summed = lax.psum_scatter(
        jnp.dot(normed, flat_weight, preferred_element_type=jnp.float32).astype(jnp.bfloat16),
        "req",
        scatter_dimension=0,
        tiled=True,
    ).astype(jnp.float32)
    split_at = summed.shape[1] // 2
    hidden = (jax.nn.silu(summed[:, :split_at]) * summed[:, split_at:]).astype(jnp.bfloat16)
    return (hidden, cache_new)


def solution(mesh):
    placed = (
        P("req"),
        P("req", "mdl"),
        P("req", None, "mdl"),
        P(),
        P("req", None, None, "mdl"),
        P(None, "req"),
        P("mdl", "req"),
        P("req"),
        P("req", None, "mdl"),
    )
    return jax.shard_map(
        on_device,
        mesh=mesh,
        in_specs=placed,
        out_specs=(P("req", "mdl"), P("req", None, None, "mdl")),
        check_vma=False,
    )
```

profile of v0, /device:TPU:0, one launch (start us, length us, event | category | flops | bytes accessed | tf_op | source)
XLA Modules:
  0.0 327.5 jit_solution(5003735953313754061)
XLA Ops:
  7.2 0.0 copy-start
  7.2 0.0 all-gather.2.cloned.1.call-start
  7.2 0.9 fusion.16
  8.1 0.7 fusion.15
  8.8 0.8 fusion.13
  9.6 1.2 fusion.21
  10.8 0.1 fusion.8
  10.9 0.2 fusion.4
  11.1 0.1 copy.24
  11.2 0.7 copy.43
  11.9 0.0 all-gather.2.cloned.1.call-update
  11.9 0.0 copy-start.8
  11.9 0.0 copy-start.4
  11.9 0.0 all-reduce.3.cloned.1.call-start
  12.0 47.6 %all-gather.2.cloned.1.call-done = bf16[1024,1024]{1,0:T(8,128)(2,1)} async-done(((bf16[64,1024]{1,0:T(8,128)(2,1)}), bf16[1024,1024]{1,0:T(8,128)(2,1)}) %all-gather.2.cloned.1.call-update) | async-done | bytes 2097168 | tf_op jit(solution)/shard_map/all_gather | solution.py:64
  59.6 0.0 copy-done
  59.6 3.8 %convolution_convert_fusion.1 = bf16[1024,512]{1,0:T(8,128)(2,1)} fusion(bf16[1024,1024]{1,0:T(8,128)(2,1)} %all-gather.2.cloned.1.call-done, bf16[1024,512]{1,0:T(8,128)(2,1)S(1)} %copy-done), kind=kOutput, calls=%fused_computation.5 | convolution fusion | flops 1074266112 | bytes 4194304 | tf_op jit(solution)/shard_map/dot_general | solution.py:63
  63.4 0.0 all-reduce.3.cloned.1.call-update
  63.4 0.0 reduce-scatter.2.cloned.1.call-start
  63.5 0.0 copy-done.8
  63.5 61.8 %all-reduce.3.cloned.1.call-done = bf16[1024,512]{1,0:T(8,128)(2,1)} async-done(((bf16[1024,512]{1,0:T(8,128)(2,1)}), bf16[1024,512]{1,0:T(8,128)(2,1)}) %all-reduce.3.cloned.1.call-update) | async-done | bytes 1048592 | tf_op jit(solution)/shard_map/psum | solution.py:69
  125.3 0.0 copy-done.4
  125.3 0.0 copy-start.5
  125.3 1.7 multiply_reduce_fusion
  127.1 40.6 %psum.15 = f32[1024]{0:T(1024)S(1)} all-reduce(f32[1024]{0:T(1024)S(1)} %multiply_reduce_fusion), channel_id=1, replica_groups=mesh['req'=16,'mdl'=8] {'req'}, use_global_device_ids=true, to_apply=%region_4.5 | all-reduce | flops 1024 | bytes 8192 | tf_op jit(solution)/shard_map/psum | solution.py:73
  167.6 0.0 copy-done.5
  167.7 14.8 %convolution_convert_fusion = bf16[1024,7392]{1,0:T(8,128)(2,1)} fusion(bf16[512,7392]{0,1:T(8,128)(2,1)} %bitcast.142, bf16[1024,512]{1,0:T(8,128)(2,1)S(1)} %copy-done.5, bf16[1024,512]{1,0:T(8,128)(2,1)S(1)} %copy-done.4, f32[512]{0:T(512)S(1)} %convert_element_type.46, f32[1024]{0:T(1024)S(1)} %add_rsqrt_fusion), kind=kOutput, calls=%fused_computation.1 | convolution fusion | flops 7761788928 | bytes 24811520 | tf_op jit(solution)/shard_map/dot_general | solution.py:79
  182.4 0.0 copy-start.11
  182.4 0.0 copy-start.3
  182.4 0.0 copy-start.7
  182.4 0.0 copy-start.10
  182.4 0.0 copy-start.9
  182.4 0.0 copy-start.6
  182.4 0.0 copy-start.2
  182.5 0.0 reduce-scatter.2.cloned.1.call-update
  182.5 0.6 copy-done.11
  183.1 0.6 dynamic-slice.6
  184.3 0.2 dynamic-update-slice.3
  184.5 36.8 %all-reduce = bf16[1024]{0:T(1024)(128)(2,1)S(1)} all-reduce(bf16[1024]{0:T(1024)(128)(2,1)S(1)} %dynamic-update-slice.3), channel_id=1, replica_groups=mesh['req'=16,'mdl'=8] {'req'}, use_global_device_ids=true, to_apply=%add | all-reduce | flops 1024 | bytes 4096
  221.3 0.0 copy-done.3
  221.3 0.7 fusion.20
  222.0 0.7 fusion.19
  222.7 0.7 fusion.17
  223.4 0.7 fusion.18
  224.2 0.0 copy-done.7
  224.2 0.1 add_add_fusion.1
  224.3 4.4 %compare_select_fusion.2 = (s32[1024,1]{0,1:T(1,128)S(1)}, s32[1024,1]{0,1:T(1,128)S(1)}) fusion(s32[]{:T(128)} %bitcast.73, s32[]{:T(128)} %bitcast.74, s32[]{:T(128)} %bitcast.75, s32[]{:T(128)} %bitcast.76, s32[]{:T(128)} %bitcast.77, s32[]{:T(128)} %bitcast.79, s32[]{:T(128)} %bitcast.78, s32[1024,1]{0,1:T(1,128)S(1)} %bitcast.141, ...), kind=kLoop, calls=%fused_computation.89 | loop fusion | flops 14336 | bytes 16412 | tf_op jit(solution)/shard_map/jit(_take)/gather | solution.py:57
  228.6 0.7 compare_reduce_fusion.56
  229.4 35.7 %compare_select_fusion.8 = s32[1024]{0:T(1024)S(1)} fusion(bf16[1024]{0:T(1024)(128)(2,1)S(1)} %all-reduce, pred[1024]{0:T(1024)(128)(4,1)S(1)} %get-tuple-element.70, pred[1024]{0:T(1024)(128)(4,1)S(1)} %get-tuple-element.69, pred[1024]{0:T(1024)(128)(4,1)S(1)} %get-tuple-element.68, pred[1024]{0:T(1024)(128)(4,1)S(1)} %get-tuple-element.67, ...), kind=kLoop, calls=%fused_computation.97 | loop fusion | flops 79872 | bytes 72968 | tf_op jit(solution)/shard_map/select_n | solution.py:62
  265.1 0.0 copy-done.10
  265.1 0.1 multiply_reduce_fusion.1
  265.2 0.0 copy-done.9
  265.2 0.1 and_reduce_fusion
  265.3 0.0 copy-done.6
  265.3 23.3 %all_gather.11 = bf16[1024,2,128]{2,1,0:T(2,128)(2,1)S(1)} all-gather(bf16[64,2,128]{2,1,0:T(2,128)(2,1)S(1)} %copy-done.6), channel_id=1, replica_groups=mesh['req'=16,'mdl'=8] {'req'}, dimensions={0}, use_global_device_ids=true | all-gather | bytes 557056 | tf_op jit(solution)/shard_map/all_gather | solution.py:52
  288.6 0.0 copy-done.2
  288.6 29.9 %scatter_fusion = bf16[128,2,128]{2,1,0:T(2,128)(2,1)S(1)} fusion(bf16[128,2,128]{2,1,0:T(2,128)(2,1)S(1)} %bitcast.134, s32[1024]{0:T(1024)S(1)} %broadcast_select_fusion, bf16[1024,2,128]{2,1,0:T(2,128)(2,1)S(1)} %all_gather.11), kind=kCustom, calls=%fused_computation | custom fusion | bytes 1576960
  318.5 0.0 copy-start.1
  318.6 0.0 reduce-scatter.2.cloned.1.call-done
  318.6 1.3 convert_element_type.49
  319.9 1.1 fusion.7
  321.0 0.0 copy-done.1
  (6 shorter events, 0.0 us)
Async XLA Ops:
  7.2 52.4 %copy-start = (bf16[1024,512]{1,0:T(8,128)(2,1)S(1)}, bf16[1024,512]{1,0:T(8,128)(2,1)}, u32[]{:S(2)}) copy-start(bf16[1024,512]{1,0:T(8,128)(2,1)} %param.17) | copy-start | bytes 3145732
  7.2 52.4 %all-gather.2.cloned.1.call-start = ((), (), s32[]{:S(2)}) async-start(), calls=%async_computation.1 | async-start | bytes 2228224 | tf_op jit(solution)/shard_map/all_gather | solution.py:64
  11.9 51.6 %copy-start.8 = (bf16[512]{0:T(512)(128)(2,1)S(1)}, bf16[512]{0:T(512)(128)(2,1)}, u32[]{:S(2)}) copy-start(bf16[512]{0:T(512)(128)(2,1)} %param.18) | copy-start | bytes 3076
  11.9 113.4 %copy-start.4 = (bf16[1024,512]{1,0:T(8,128)(2,1)S(1)}, bf16[1024,512]{1,0:T(8,128)(2,1)}, u32[]{:S(2)}) copy-start(bf16[1024,512]{1,0:T(8,128)(2,1)} %param.16) | copy-start | bytes 3145732
  11.9 113.4 %all-reduce.3.cloned.1.call-start = ((), (), s32[]{:S(2)}) async-start(), calls=%async_computation.2 | async-start | bytes 2097152 | tf_op jit(solution)/shard_map/psum | solution.py:69
  63.4 255.1 %reduce-scatter.2.cloned.1.call-start = ((), (), s32[]{:S(2)}) async-start(), calls=%async_computation.3 | async-start | bytes 16154624 | tf_op jit(solution)/shard_map/reduce_scatter | solution.py:78
  125.3 42.3 %copy-start.5 = (bf16[1024,512]{1,0:T(8,128)(2,1)S(1)}, bf16[1024,512]{1,0:T(8,128)(2,1)}, u32[]{:S(2)}) copy-start(bf16[1024,512]{1,0:T(8,128)(2,1)} %all-reduce.3.cloned.1.call-done) | copy-start | bytes 3145732
  182.4 0.7 copy-start.11
  182.4 38.9 %copy-start.3 = (s32[64]{0:T(128)S(1)}, s32[64]{0:T(128)}, u32[]{:S(2)}) copy-start(s32[64]{0:T(128)} %param.14) | copy-start | bytes 772
  182.4 41.8 %copy-start.7 = (s32[8,128]{1,0:T(8,128)S(1)}, s32[8,128]{1,0:T(8,128)}, u32[]{:S(2)}) copy-start(s32[8,128]{1,0:T(8,128)} %constant.119.clone.1) | copy-start | bytes 12292
  182.4 82.7 %copy-start.10 = (s32[2]{0:T(128)S(1)}, s32[2]{0:T(128)}, u32[]{:S(2)}) copy-start(s32[2]{0:T(128)} %constant.129) | copy-start | bytes 28
  182.4 82.8 %copy-start.9 = (s32[2]{0:T(128)S(1)}, s32[2]{0:T(128)}, u32[]{:S(2)}) copy-start(s32[2]{0:T(128)} %constant.132) | copy-start | bytes 28
  182.4 82.9 %copy-start.6 = (bf16[64,2,128]{2,1,0:T(2,128)(2,1)S(1)}, bf16[64,2,128]{2,1,0:T(2,128)(2,1)}, u32[]{:S(2)}) copy-start(bf16[64,2,128]{2,1,0:T(2,128)(2,1)} %param.13) | copy-start | bytes 98308
  182.4 106.1 %copy-start.2 = (bf16[8,16,2,128]{3,2,1,0:T(2,128)(2,1)S(1)}, bf16[8,16,2,128]{3,2,1,0:T(2,128)(2,1)}, u32[]{:S(2)}) copy-start(bf16[8,16,2,128]{3,2,1,0:T(2,128)(2,1)} %param.15) | copy-start | bytes 196612
  318.5 2.5 copy-start.1
Sparse Core Ops, SparseCore 0:
  12.0 47.5 all-gather.1
  63.6 61.7 all-reduce.2
  182.6 99.0 reduce-scatter.1
where the time goes:
time: 328 us
  waiting for transfers between devices  110 us (34%)
  blocking collectives  101 us (31%)
  other arithmetic  46.8 us (14%)
  local copies, waits for them, and re-layouts  35.9 us (11%)
  matrix products  20 us (6%)
  between operations  14.6 us (4%)
    psum x1, waiting for transfers between devices, on_device(): lax.psum(partial_value.astype(jnp.bfloat16), 'mdl').astype(jnp.float32)  61.8 us
    all_gather x1, waiting for transfers between devices, on_device(): lax.all_gather(attended, 'req', axis=0, tiled=True)  47.6 us
    psum x1, blocking collectives, on_device(): totals = lax.psum(squares, 'req')  40.6 us
    unnamed x1, blocking collectives  36.8 us
    select_n x2, other arithmetic, on_device(): cache_new = paged_cache.at[target, offsets].set(every_pair, mode='drop')  35.7 us
    unnamed x29, local copies, waits for them, and re-layouts  32.1 us
    all_gather x1, blocking collectives, on_device(): lax.all_gather(keys_values, 'req', axis=0, tiled=True)  23.3 us
    dot_general x1, matrix products, on_device(): jnp.dot(normed, flat_weight, preferred_element_type=jnp.float32)  14.8 us
  transfers between devices with their start and end apart: 3, of which 2 were waited for; matrix products, arithmetic and copies ran while one was open for 23% of the time, Pallas kernels for 0%

commit v1 on v0

--- a/solution.py
+++ b/solution.py
@@ -8,6 +8,16 @@
 QPK = 8
 PAGE = 16
 EPSILON = 1e-06
+
+
+def open_leaves(here_x):
+    return lax.all_to_all(
+        jnp.concatenate(lax.axis_size("req") * [here_x], 0),
+        "req",
+        concat_axis=0,
+        split_axis=0,
+        tiled=True,
+    )
 
 
 def attention_block(query_rows, pair_rows, seg_rows):
@@ -60,11 +70,7 @@
     target = jnp.where(writable, target, local_pages)
     offsets = jnp.arange(slot_count, dtype=jnp.int32) % PAGE
     cache_new = paged_cache.at[target, offsets].set(every_pair, mode="drop")
-    partial_value = jnp.dot(
-        lax.all_gather(attended, "req", axis=0, tiled=True),
-        out_weight,
-        preferred_element_type=jnp.float32,
-    )
+    partial_value = jnp.dot(open_leaves(attended), out_weight, preferred_element_type=jnp.float32)
     gain_row = norm_gain.astype(jnp.float32)
     stream = residual.astype(jnp.float32) + lax.psum(
         partial_value.astype(jnp.bfloat16), "mdl"

time: 328 us -> 315 us (0.960)
  waiting for transfers between devices: 110 us -> 60.8 us
  blocking collectives: 101 us -> 137 us
    all_gather x1 -> x0, waiting for transfers between devices: 47.6 us -> none  [on_device(): lax.all_gather(attended, 'req', axis=0, tiled=True)]
    all_to_all x0 -> x1, blocking collectives: none -> 36.2 us  [open_leaves(): lax.all_to_all(jnp.concatenate(lax.axis_size('req') * [here_x], 0), 'req'...]
    unnamed x29 -> x43, local copies, waits for them, and re-layouts: 32.1 us -> 31.7 us
  transfers between devices with their start and end apart: 3 -> 2, of which waited for: 2 -> 1; matrix products, arithmetic and copies ran while one was open for 23% -> 24% of each run, Pallas kernels for 0% -> 0%
where the time goes in v1:
time: 315 us; the launch traced here: 314 us
  blocking collectives  137 us (43%)
  waiting for transfers between devices  60.8 us (19%)
  other arithmetic  46.8 us (15%)
  local copies, waits for them, and re-layouts  35.5 us (11%)
  matrix products  18.4 us (6%)
  between operations  15 us (5%)
    psum x1, waiting for transfers between devices, on_device(): lax.psum(partial_value.astype(jnp.bfloat16), 'mdl').astype(jnp.float32)  60.8 us
    psum x1, blocking collectives, on_device(): totals = lax.psum(squares, 'req')  40.6 us
    unnamed x1, blocking collectives  36.7 us
    all_to_all x1, blocking collectives, open_leaves(): lax.all_to_all(jnp.concatenate(lax.axis_size('req') * [here_x], 0), 'req'...  36.2 us
    select_n x2, other arithmetic, on_device(): cache_new = paged_cache.at[target, offsets].set(every_pair, mode='drop')  35.7 us
    unnamed x43, local copies, waits for them, and re-layouts  31.7 us
    all_gather x1, blocking collectives, on_device(): lax.all_gather(keys_values, 'req', axis=0, tiled=True)  23.4 us
    dot_general x1, matrix products, on_device(): jnp.dot(normed, flat_weight, preferred_element_type=jnp.float32)  14.8 us
  transfers between devices with their start and end apart: 2, of which 1 were waited for; matrix products, arithmetic and copies ran while one was open for 24% of the time, Pallas kernels for 0%

profile of v1, /device:TPU:0, one launch (start us, length us, event | category | flops | bytes accessed | tf_op | source)
XLA Modules:
  0.0 313.6 jit_solution(17197051607608939252)
XLA Ops:
  7.2 0.0 copy-start
  7.2 0.0 all-reduce.3.cloned.1.call-start
  7.2 0.7 fusion.15
  8.0 0.8 fusion.13
  8.8 0.9 fusion.16
  9.7 1.2 fusion.21
  10.8 0.1 fusion.8
  10.9 0.2 fusion.4
  11.2 0.1 copy.24
  11.7 36.2 %all_to_all.12 = bf16[16,64,1024]{2,1,0:T(8,128)(2,1)S(1)} all-to-all(bf16[16,64,1024]{2,1,0:T(8,128)(2,1)S(1)} %bitcast.167), channel_id=1, replica_groups=mesh['req'=16,'mdl'=8] {'req'}, dimensions={0} | all-to-all | bytes 4194304 | tf_op jit(solution)/shard_map/all_to_all | solution.py:14
  47.9 0.0 copy-done
  47.9 0.0 copy-start.8
  47.9 0.0 copy-start.4
  47.9 2.3 convolution_convert_fusion.1
  50.2 0.0 all-reduce.3.cloned.1.call-update
  50.2 0.0 reduce-scatter.2.cloned.1.call-start
  50.2 0.0 copy-done.8
  50.3 60.8 %all-reduce.3.cloned.1.call-done = bf16[1024,512]{1,0:T(8,128)(2,1)} async-done(((bf16[1024,512]{1,0:T(8,128)(2,1)}), bf16[1024,512]{1,0:T(8,128)(2,1)}) %all-reduce.3.cloned.1.call-update) | async-done | bytes 1048592 | tf_op jit(solution)/shard_map/psum | solution.py:75
  111.0 0.0 copy-done.4
  111.0 0.0 copy-start.5
  111.0 1.7 multiply_reduce_fusion
  112.8 40.6 %psum.15 = f32[1024]{0:T(1024)S(1)} all-reduce(f32[1024]{0:T(1024)S(1)} %multiply_reduce_fusion), channel_id=1, replica_groups=mesh['req'=16,'mdl'=8] {'req'}, use_global_device_ids=true, to_apply=%region_4.5 | all-reduce | flops 1024 | bytes 8192 | tf_op jit(solution)/shard_map/psum | solution.py:79
  153.4 0.0 copy-done.5
  153.4 14.8 %convolution_convert_fusion = bf16[1024,7392]{1,0:T(8,128)(2,1)} fusion(bf16[512,7392]{0,1:T(8,128)(2,1)} %bitcast.174, bf16[1024,512]{1,0:T(8,128)(2,1)S(1)} %copy-done.5, bf16[1024,512]{1,0:T(8,128)(2,1)S(1)} %copy-done.4, f32[512]{0:T(512)S(1)} %convert_element_type.46, f32[1024]{0:T(1024)S(1)} %add_rsqrt_fusion), kind=kOutput, calls=%fused_computation.1 | convolution fusion | flops 7761788928 | bytes 24811520 | tf_op jit(solution)/shard_map/dot_general | solution.py:85
  168.1 0.0 copy-start.11
  168.1 0.0 copy-start.3
  168.1 0.0 copy-start.7
  168.1 0.0 copy-start.10
  168.1 0.0 copy-start.9
  168.1 0.0 copy-start.6
  168.2 0.0 copy-start.2
  168.2 0.0 reduce-scatter.2.cloned.1.call-update
  168.2 0.6 copy-done.11
  168.8 0.6 dynamic-slice.6
  170.0 0.2 dynamic-update-slice.3
  170.3 36.7 %all-reduce = bf16[1024]{0:T(1024)(128)(2,1)S(1)} all-reduce(bf16[1024]{0:T(1024)(128)(2,1)S(1)} %dynamic-update-slice.3), channel_id=1, replica_groups=mesh['req'=16,'mdl'=8] {'req'}, use_global_device_ids=true, to_apply=%add | all-reduce | flops 1024 | bytes 4096
  206.9 0.0 copy-done.3
  206.9 0.7 fusion.20
  207.6 0.7 fusion.19
  208.3 0.7 fusion.17
  209.1 0.7 fusion.18
  209.8 0.0 copy-done.7
  209.8 0.1 add_add_fusion.1
  209.9 4.4 %compare_select_fusion.2 = (s32[1024,1]{0,1:T(1,128)S(1)}, s32[1024,1]{0,1:T(1,128)S(1)}) fusion(s32[]{:T(128)} %bitcast.75, s32[]{:T(128)} %bitcast.76, s32[]{:T(128)} %bitcast.77, s32[]{:T(128)} %bitcast.78, s32[]{:T(128)} %bitcast.79, s32[]{:T(128)} %bitcast.81, s32[]{:T(128)} %bitcast.80, s32[1024,1]{0,1:T(1,128)S(1)} %bitcast.173, ...), kind=kLoop, calls=%fused_computation.104 | loop fusion | flops 14336 | bytes 16412 | tf_op jit(solution)/shard_map/jit(_take)/gather | solution.py:67
  214.3 0.7 compare_reduce_fusion.56
  215.0 35.7 %compare_select_fusion.8 = s32[1024]{0:T(1024)S(1)} fusion(bf16[1024]{0:T(1024)(128)(2,1)S(1)} %all-reduce, pred[1024]{0:T(1024)(128)(4,1)S(1)} %get-tuple-element.70, pred[1024]{0:T(1024)(128)(4,1)S(1)} %get-tuple-element.69, pred[1024]{0:T(1024)(128)(4,1)S(1)} %get-tuple-element.68, pred[1024]{0:T(1024)(128)(4,1)S(1)} %get-tuple-element.67, ...), kind=kLoop, calls=%fused_computation.112 | loop fusion | flops 79872 | bytes 72968 | tf_op jit(solution)/shard_map/select_n | solution.py:72
  250.7 0.0 copy-done.10
  250.7 0.1 multiply_reduce_fusion.1
  250.8 0.0 copy-done.9
  250.8 0.1 and_reduce_fusion
  250.9 0.0 copy-done.6
  250.9 23.4 %all_gather.7 = bf16[1024,2,128]{2,1,0:T(2,128)(2,1)S(1)} all-gather(bf16[64,2,128]{2,1,0:T(2,128)(2,1)S(1)} %copy-done.6), channel_id=1, replica_groups=mesh['req'=16,'mdl'=8] {'req'}, dimensions={0}, use_global_device_ids=true | all-gather | bytes 557056 | tf_op jit(solution)/shard_map/all_gather | solution.py:62
  274.4 0.0 copy-done.2
  274.4 29.9 %scatter_fusion = bf16[128,2,128]{2,1,0:T(2,128)(2,1)S(1)} fusion(bf16[128,2,128]{2,1,0:T(2,128)(2,1)S(1)} %bitcast.166, s32[1024]{0:T(1024)S(1)} %broadcast_select_fusion, bf16[1024,2,128]{2,1,0:T(2,128)(2,1)S(1)} %all_gather.7), kind=kCustom, calls=%fused_computation | custom fusion | bytes 1576960
  304.3 0.0 copy-start.1
  304.3 0.0 reduce-scatter.2.cloned.1.call-done
  304.4 1.3 convert_element_type.49
  305.7 1.1 fusion.7
  306.8 0.0 copy-done.1
  (22 shorter events, 0.3 us)
Async XLA Ops:
  7.2 40.7 %copy-start = (bf16[1024,512]{1,0:T(8,128)(2,1)S(1)}, bf16[1024,512]{1,0:T(8,128)(2,1)}, u32[]{:S(2)}) copy-start(bf16[1024,512]{1,0:T(8,128)(2,1)} %param.17) | copy-start | bytes 3145732
  7.2 103.9 %all-reduce.3.cloned.1.call-start = ((), (), s32[]{:S(2)}) async-start(), calls=%async_computation.2 | async-start | bytes 2097152 | tf_op jit(solution)/shard_map/psum | solution.py:75
  47.9 2.4 copy-start.8
  47.9 63.2 %copy-start.4 = (bf16[1024,512]{1,0:T(8,128)(2,1)S(1)}, bf16[1024,512]{1,0:T(8,128)(2,1)}, u32[]{:S(2)}) copy-start(bf16[1024,512]{1,0:T(8,128)(2,1)} %param.16) | copy-start | bytes 3145732
  50.2 254.2 %reduce-scatter.2.cloned.1.call-start = ((), (), s32[]{:S(2)}) async-start(), calls=%async_computation.3 | async-start | bytes 16154624 | tf_op jit(solution)/shard_map/reduce_scatter | solution.py:84
  111.0 42.3 %copy-start.5 = (bf16[1024,512]{1,0:T(8,128)(2,1)S(1)}, bf16[1024,512]{1,0:T(8,128)(2,1)}, u32[]{:S(2)}) copy-start(bf16[1024,512]{1,0:T(8,128)(2,1)} %all-reduce.3.cloned.1.call-done) | copy-start | bytes 3145732
  168.1 0.7 copy-start.11
  168.1 38.8 %copy-start.3 = (s32[64]{0:T(128)S(1)}, s32[64]{0:T(128)}, u32[]{:S(2)}) copy-start(s32[64]{0:T(128)} %param.14) | copy-start | bytes 772
  168.1 41.7 %copy-start.7 = (s32[8,128]{1,0:T(8,128)S(1)}, s32[8,128]{1,0:T(8,128)}, u32[]{:S(2)}) copy-start(s32[8,128]{1,0:T(8,128)} %constant.119.clone.1) | copy-start | bytes 12292
  168.1 82.6 %copy-start.10 = (s32[2]{0:T(128)S(1)}, s32[2]{0:T(128)}, u32[]{:S(2)}) copy-start(s32[2]{0:T(128)} %constant.129) | copy-start | bytes 28
  168.1 82.7 %copy-start.9 = (s32[2]{0:T(128)S(1)}, s32[2]{0:T(128)}, u32[]{:S(2)}) copy-start(s32[2]{0:T(128)} %constant.132) | copy-start | bytes 28
  168.1 82.8 %copy-start.6 = (bf16[64,2,128]{2,1,0:T(2,128)(2,1)S(1)}, bf16[64,2,128]{2,1,0:T(2,128)(2,1)}, u32[]{:S(2)}) copy-start(bf16[64,2,128]{2,1,0:T(2,128)(2,1)} %param.13) | copy-start | bytes 98308
  168.2 106.2 %copy-start.2 = (bf16[8,16,2,128]{3,2,1,0:T(2,128)(2,1)S(1)}, bf16[8,16,2,128]{3,2,1,0:T(2,128)(2,1)}, u32[]{:S(2)}) copy-start(bf16[8,16,2,128]{3,2,1,0:T(2,128)(2,1)} %param.15) | copy-start | bytes 196612
  304.3 2.5 copy-start.1
Sparse Core Ops, SparseCore 0:
  50.3 60.6 all-reduce.2
  168.3 98.8 reduce-scatter.1
